TPU v7x, 32 devices: a whole 2x2x4 slice. The times are simulated.
32 devices in a mesh: dp: 4 (over y, x), expert: 8 (over z, core).
Axes of the slice: x: 2, y: 2, z: 4, core: 2. Of those that a mesh axis runs over, the one named last changes fastest.
Arguments:
- tokens: bfloat16 [4096, 1024], P(('dp', 'expert')), may hold values from -12 to 12
- routes: int32 [4096, 8], P(('dp', 'expert')), may hold values from 0 to 31, all different within a row; in each aligned block of 128 rows (0 to 127, 128 to 255, ...) at most 48 rows name the same one
- gate_weights: float32 [4096, 8], P(('dp', 'expert')), may hold values from 0.05 to 0.25
- cotangent: bfloat16 [4096, 1024], P(('dp', 'expert')), may hold values from -12 to 12
- w_gate_up: bfloat16 [1024, 32, 768], P(None, 'expert'), may hold values from -0.1875 to 0.1875
- w_down: bfloat16 [1024, 32, 384], P(None, 'expert'), may hold values from -0.3125 to 0.3125
Outputs:
- layer_out: bfloat16 [4096, 1024], P(('dp', 'expert'))
- grad_tokens: bfloat16 [4096, 1024], P(('dp', 'expert'))
- grad_gate_up: bfloat16 [1024, 32, 768], P('dp', 'expert')
- grad_down: bfloat16 [1024, 32, 384], P('dp', 'expert')
Inputs may be any that keep to these rules, and one draw needn't show every extreme that they name: `routes`: each row names 8 different experts. Among the 128 rows of one device no expert is named more than 48 times, and in some device's rows an expert is named exactly 48 times.
All inputs are finite; a program needn't handle non-finite values.
Results may differ from a plain program's by a relative error of at most 0.015.
Values may be sent and summed in bfloat16 or wider, within the bound.
No kernel may reach another device: no remote copies, remote signals or barrier semaphores. Data moves between devices by JAX's collectives and lax.ppermute only.
A program may use at most 128 MiB of HBM per device.

v0:
```python
import jax
import jax.numpy as jnp
from jax import lax
from jax.sharding import PartitionSpec as P


def split_parts(projected, hidden_units):
    gate_part = projected[..., :hidden_units]
    up_part = projected[..., hidden_units:]
    sigma = jax.nn.sigmoid(gate_part)
    return (gate_part, up_part, sigma)


def forward_local(received, w_gate_up, w_down, hidden_units):
    projected = jnp.einsum(
        "slmd,dlf->slmf", received, w_gate_up, preferred_element_type=jnp.float32
    )
    gate_part, up_part, sigma = split_parts(projected, hidden_units)
    hidden_fwd = (gate_part * sigma * up_part).astype(jnp.bfloat16)
    expert_out = jnp.einsum(
        "slmh,dlh->slmd", hidden_fwd, w_down, preferred_element_type=jnp.float32
    ).astype(jnp.bfloat16)
    return (projected, expert_out)


def backward_local(projected, received_cot, w_gate_up, w_down, hidden_units):
    gate_part, up_part, sigma = split_parts(projected, hidden_units)
    hidden = (gate_part * sigma * up_part).astype(jnp.bfloat16)
    d_hidden = jnp.einsum(
        "slmd,dlh->slmh", received_cot, w_down, preferred_element_type=jnp.float32
    )
    d_gate = d_hidden * up_part * sigma * (1.0 + gate_part * (1.0 - sigma))
    d_up = d_hidden * gate_part * sigma
    d_proj = jnp.concatenate([d_gate, d_up], axis=-1).astype(jnp.bfloat16)
    slot_grads = jnp.einsum(
        "slmf,dlf->slmd", d_proj, w_gate_up, preferred_element_type=jnp.float32
    ).astype(jnp.bfloat16)
    return (hidden, d_proj, slot_grads)


def per_device(tokens, routes, gate_weights, cotangent, w_gate_up, w_down):
    tok_dev, active = routes.shape
    model_width = tokens.shape[1]
    exp_dev = w_down.shape[1]
    hidden_units = w_down.shape[2]
    expert_peers = lax.axis_size("expert")
    experts_all = exp_dev * expert_peers
    capacity = 3 * tok_dev * active // (2 * experts_all)
    assigned = tok_dev * active
    slots_all = experts_all * capacity
    flat_routes = routes.reshape(assigned)
    onehot = (flat_routes[:, None] == jnp.arange(experts_all, dtype=jnp.int32)[None, :]).astype(
        jnp.int32
    )
    slot_rank = jnp.sum((jnp.cumsum(onehot, axis=0) - 1) * onehot, axis=1)
    slot_index = flat_routes * capacity + slot_rank
    source_of = (
        jnp.zeros((slots_all,), jnp.int32).at[slot_index].set(jnp.arange(assigned, dtype=jnp.int32))
    )
    filled = jnp.zeros((slots_all,), jnp.int32).at[slot_index].set(1) > 0
    token_of = source_of // active
    empty_row = jnp.zeros((), jnp.bfloat16)
    slot_shape = (expert_peers, exp_dev, capacity, model_width)
    x_slots = jnp.where(filled[:, None], tokens[token_of], empty_row).reshape(slot_shape)
    flat_gates = gate_weights.reshape(assigned)
    weighted = (flat_gates[source_of][:, None] * cotangent[token_of].astype(jnp.float32)).astype(
        jnp.bfloat16
    )
    cot_slots = jnp.where(filled[:, None], weighted, empty_row).reshape(slot_shape)
    received = lax.all_to_all(x_slots, "expert", split_axis=0, concat_axis=0, tiled=True)
    received_c = lax.all_to_all(cot_slots, "expert", split_axis=0, concat_axis=0, tiled=True)
    projected_f, out_local = forward_local(received, w_gate_up, w_down, hidden_units)
    hidden_local, d_proj_local, grads_local = backward_local(
        projected_f, received_c, w_gate_up, w_down, hidden_units
    )
    back_out = lax.all_to_all(out_local, "expert", split_axis=0, concat_axis=0, tiled=True)
    back_grad = lax.all_to_all(grads_local, "expert", split_axis=0, concat_axis=0, tiled=True)
    per_assign = back_out.reshape(slots_all, model_width)[slot_index].reshape(
        tok_dev, active, model_width
    )
    layer_out = jnp.sum(per_assign.astype(jnp.float32) * gate_weights[:, :, None], axis=1).astype(
        jnp.bfloat16
    )
    grad_assign = back_grad.reshape(slots_all, model_width)[slot_index].reshape(
        tok_dev, active, model_width
    )
    grad_tokens = jnp.sum(grad_assign.astype(jnp.float32), axis=1).astype(jnp.bfloat16)
    term_gu = jnp.einsum(
        "slmd,slmf->dlf", received, d_proj_local, preferred_element_type=jnp.float32
    )
    term_dn = jnp.einsum(
        "slmd,slmh->dlh", received_c, hidden_local, preferred_element_type=jnp.float32
    )
    summed = lax.psum_scatter(
        jnp.concatenate([term_gu, term_dn], axis=2).astype(jnp.bfloat16),
        "dp",
        scatter_dimension=0,
        tiled=True,
    ).astype(jnp.float32)
    grad_gate_up = summed[:, :, : 2 * hidden_units].astype(jnp.bfloat16)
    grad_down = summed[:, :, 2 * hidden_units :].astype(jnp.bfloat16)
    return (layer_out, grad_tokens, grad_gate_up, grad_down)


def solution(mesh):
    in_specs = (
        P(("dp", "expert"), None),
        P(("dp", "expert"), None),
        P(("dp", "expert"), None),
        P(("dp", "expert"), None),
        P(None, "expert", None),
        P(None, "expert", None),
    )
    out_specs = (
        P(("dp", "expert"), None),
        P(("dp", "expert"), None),
        P("dp", "expert", None),
        P("dp", "expert", None),
    )
    return jax.shard_map(
        per_device, mesh=mesh, in_specs=in_specs, out_specs=out_specs, check_vma=False
    )
```

profile of v0, /device:TPU:0, one launch (start us, length us, event | category | flops | bytes accessed | tf_op | source)
XLA Modules:
  0.0 419.5 jit_solution(14420779065767338540)
XLA Ops:
  7.2 0.0 copy-start
  7.2 0.8 broadcast_multiply_fusion
  8.0 0.9 copy.37
  8.9 0.1 eq.29
  9.0 0.1 eq.25
  9.1 0.1 copy.36
  9.2 0.1 mul.66
  9.3 9.0 %reduce-window.6 = s32[32,8,128]{2,1,0:T(8,128)S(1)} reduce-window(s32[32,8,128]{2,1,0:T(8,128)S(1)} %fusion.36, s32[]{:T(128)} %constant.13.clone.1), window={size=1x1x128 pad=0_0x0_0x127_0}, to_apply=%region_0.0 | reduce-window | flops 4161536 | bytes 262148 | tf_op jit(solution)/shard_map/reduce-window
  18.3 0.1 slice.38
  18.4 0.1 copy.39
  18.6 0.1 copy.40
  18.7 0.1 add_add_fusion
  18.9 4.3 %scatter_custom_fusion.1 = s32[1536]{0:T(1024)S(1)} fusion(s32[1024]{0:T(1024)S(1)} %bitcast.72, s32[1024]{0:T(1024)S(1)} %iota.11, s32[]{:T(128)} %constant.13.clone.1), kind=kCustom, calls=%fused_computation.64 | custom fusion | bytes 6148 | tf_op jit(solution)/shard_map/scatter | solution.py:58
  23.2 0.8 copy.45
  24.0 0.1 reshape.96
  24.1 0.0 copy-start.1
  24.1 5.9 %gather_fusion.2 = f32[1536]{0:T(1024)S(1)} fusion(f32[1024]{0:T(1024)S(1)} %reshape.96, s32[2048]{0:T(1024)S(1)} %get-tuple-element.23), kind=kCustom, calls=%fused_computation.2 | custom fusion | bytes 18432 | tf_op jit(solution)/shard_map/gather | solution.py:66
  30.0 0.1 mul.72
  30.1 4.3 %scatter_custom_fusion = s32[1536]{0:T(1024)S(1)} fusion(s32[1024]{0:T(1024)S(1)} %bitcast.73, s32[1024]{0:T(1024)S(1)} %broadcast.84, s32[]{:T(128)} %constant.13.clone.1), kind=kCustom, calls=%fused_computation.67 | custom fusion | bytes 6148 | tf_op jit(solution)/shard_map/scatter | solution.py:60
  34.4 0.1 broadcast_in_dim.38
  34.5 0.0 copy-done.1
  34.5 5.8 %gather_fusion.3 = bf16[1536,1024]{1,0:T(8,128)(2,1)} fusion(bf16[128,1024]{1,0:T(8,128)(2,1)S(1)} %copy-done.1, s32[2048]{0:T(1024)S(1)} %get-tuple-element.24), kind=kCustom, calls=%fused_computation.3 | custom fusion | bytes 6297600 | tf_op jit(solution)/shard_map/gather | solution.py:66
  40.3 8.8 %gather_fusion = bf16[1536,1024]{1,0:T(8,128)(2,1)} fusion(bf16[128,1024]{1,0:T(8,128)(2,1)} %param.6, s32[2048]{0:T(1024)S(1)} %get-tuple-element.24), kind=kCustom, calls=%fused_computation | custom fusion | bytes 6297600 | tf_op jit(solution)/shard_map/gather | solution.py:64
  49.1 4.8 %fusion.8 = (bf16[8,4,48,1024]{3,2,1,0:T(8,128)(2,1)}, bf16[8,4,48,1024]{3,2,1,0:T(8,128)(2,1)S(1)}) fusion(bf16[8,4,48,1024]{3,2,1,0:T(8,128)(2,1)} %bitcast.67, f32[8,4,48]{2,1,0:T(4,128)S(1)} %mul.72, pred[8,4,48]{2,1,0:T(4,128)(4,1)S(1)} %broadcast_in_dim.38, bf16[8,4,48,1024]{3,2,1,0:T(8,128)(2,1)} %bitcast.68), kind=kLoop, calls=%fused_computation.20 | loop fusion | flops 7864320 | bytes 12590592 | tf_op jit(solution)/shard_map/jit(_where)/select_n | solution.py:69
  53.9 77.7 %all_to_all.20 = bf16[8,4,48,1024]{3,2,1,0:T(8,128)(2,1)} all-to-all(bf16[8,4,48,1024]{3,2,1,0:T(8,128)(2,1)S(1)} %get-tuple-element.22), channel_id=1, replica_groups=mesh['dp'=4,'expert'=8] {'expert'}, dimensions={0} | all-to-all | bytes 6291456 | tf_op jit(solution)/shard_map/all_to_all | solution.py:70
  131.7 4.4 %all-to-all-start.2 = ((bf16[8,4,48,1024]{3,2,1,0:T(8,128)(2,1)}), bf16[8,4,48,1024]{3,2,1,0:T(8,128)(2,1)}, u32[]{:S(2)}, u32[]{:S(2)}) async-start(bf16[8,4,48,1024]{3,2,1,0:T(8,128)(2,1)} %get-tuple-element.21), calls=%async_computation.2 | async-start | bytes 6291456 | tf_op jit(solution)/shard_map/all_to_all | solution.py:71
  136.1 0.2 reduce-scatter.2.cloned.1.call-start
  136.4 8.5 %fusion.25 = f32[8,4,48,768]{3,2,0,1:T(8,128)} fusion(bf16[1024,4,768,1]{2,1,0,3:T(4,128)(2,1)} %bitcast.75, bf16[8,4,48,1024]{3,2,1,0:T(8,128)(2,1)} %all_to_all.20), kind=kOutput, calls=%fused_computation.43 | convolution fusion | flops 2415919104 | bytes 14155776 | tf_op jit(solution)/shard_map/slmd,dlf->slmf/dot_general | solution.py:15
  144.9 62.8 %all-to-all-done.2 = bf16[8,4,48,1024]{3,2,1,0:T(8,128)(2,1)} async-done(((bf16[8,4,48,1024]{3,2,1,0:T(8,128)(2,1)}), bf16[8,4,48,1024]{3,2,1,0:T(8,128)(2,1)}, u32[]{:S(2)}, u32[]{:S(2)}) %all-to-all-start.2) | async-done | bytes 3145760 | tf_op jit(solution)/shard_map/all_to_all | solution.py:71
  207.7 0.0 copy-done
  207.7 5.9 %fusion.20 = (bf16[8,4,48,384]{3,2,0,1:T(8,128)(2,1)S(1)}, bf16[8,4,48,384]{3,2,0,1:T(8,128)(2,1)S(1)}, bf16[8,4,48,384]{3,2,0,1:T(8,128)(2,1)S(1)}) fusion(f32[8,4,48,768]{3,2,0,1:T(8,128)} %fusion.25, bf16[1024,4,384,1]{2,1,0,3:T(4,128)(2,1)S(1)} %bitcast.66, bf16[8,4,48,1024]{3,2,1,0:T(8,128)(2,1)} %all-to-all-done.2), kind=kOutput, calls=%fused_computation.38 | convolution fusion | flops 1217396736 | bytes 14548992 | tf_op jit(solution)/shard_map/slmd,dlh->slmh/dot_general | solution.py:29
  213.5 0.0 copy-start.4
  213.5 0.0 copy-start.5
  213.5 0.0 copy-start.6
  213.6 0.0 copy-start.3
  213.6 5.0 %fusion.7 = bf16[1024,4,384]{0,2,1:T(8,128)(2,1)S(1)} fusion(bf16[8,4,48,384]{3,2,0,1:T(8,128)(2,1)S(1)} %get-tuple-element.18, bf16[8,4,48,1024]{3,2,1,0:T(8,128)(2,1)} %all-to-all-done.2), kind=kOutput, calls=%fused_computation.19 | convolution fusion | flops 1209532416 | bytes 7471104 | tf_op jit(solution)/shard_map/slmd,slmh->dlh/dot_general | solution.py:91
  218.6 0.0 copy-done.4
  218.6 0.0 copy-done.5
  218.6 0.0 copy-done.6
  218.6 0.0 copy-done.3
  218.7 3.7 fusion
  222.4 8.2 %pad_maximum_fusion = bf16[1024,4,1152]{0,2,1:T(8,128)(2,1)} fusion(bf16[1024,4,384]{0,2,1:T(8,128)(2,1)S(1)} %fusion.7, bf16[1024,4,768]{0,2,1:T(8,128)(2,1)S(1)} %fusion), kind=kLoop, calls=%fused_computation.8 | loop fusion | flops 18874368 | bytes 18874368 | tf_op jit(solution)/shard_map/concatenate | solution.py:95
  230.6 0.0 reduce-scatter.2.cloned.1.call-update
  230.6 3.1 convert_bitcast_fusion.1
  233.7 2.1 copy.44
  235.8 4.7 %all-to-all-start.1 = ((bf16[8,4,48,1024]{3,2,1,0:T(8,128)(2,1)}), bf16[8,4,48,1024]{3,2,1,0:T(8,128)(2,1)}, u32[]{:S(2)}, u32[]{:S(2)}) async-start(bf16[8,4,48,1024]{3,2,1,0:T(8,128)(2,1)} %copy.44), calls=%async_computation.1 | async-start | bytes 6291456 | tf_op jit(solution)/shard_map/all_to_all | solution.py:76
  240.4 6.4 %convert_bitcast_fusion = bf16[8,4,48,1024]{3,2,0,1:T(8,128)(2,1)S(1)} fusion(bf16[1024,4,768,1]{2,1,0,3:T(4,128)(2,1)} %bitcast.76, bf16[8,4,48,384]{3,2,0,1:T(8,128)(2,1)} %copy-done.6, bf16[8,4,48,384]{3,2,0,1:T(8,128)(2,1)} %copy-done.5), kind=kOutput, calls=%fused_computation.21 | convolution fusion | flops 2422210560 | bytes 11796480 | tf_op jit(solution)/shard_map/slmf,dlf->slmd/dot_general | solution.py:35
  246.9 2.0 copy.50
  248.8 62.9 %all-to-all-done.1 = bf16[8,4,48,1024]{3,2,1,0:T(8,128)(2,1)} async-done(((bf16[8,4,48,1024]{3,2,1,0:T(8,128)(2,1)}), bf16[8,4,48,1024]{3,2,1,0:T(8,128)(2,1)}, u32[]{:S(2)}, u32[]{:S(2)}) %all-to-all-start.1) | async-done | bytes 3145760 | tf_op jit(solution)/shard_map/all_to_all | solution.py:76
  311.7 4.5 %all-to-all-start.3 = ((bf16[8,4,48,1024]{3,2,1,0:T(8,128)(2,1)}), bf16[8,4,48,1024]{3,2,1,0:T(8,128)(2,1)}, u32[]{:S(2)}, u32[]{:S(2)}) async-start(bf16[8,4,48,1024]{3,2,1,0:T(8,128)(2,1)} %copy.50), calls=%async_computation.3 | async-start | bytes 6291456 | tf_op jit(solution)/shard_map/all_to_all | solution.py:77
  316.2 8.3 %gather_fusion.1 = bf16[1024,1024]{1,0:T(8,128)(2,1)} fusion(bf16[1536,1024]{1,0:T(8,128)(2,1)} %bitcast.9, s32[1024]{0:T(1024)S(1)} %broadcast_clamp_fusion), kind=kCustom, calls=%fused_computation.1 | custom fusion | bytes 4198400 | tf_op jit(solution)/shard_map/gather | solution.py:78
  324.5 63.2 %all-to-all-done.3 = bf16[8,4,48,1024]{3,2,1,0:T(8,128)(2,1)} async-done(((bf16[8,4,48,1024]{3,2,1,0:T(8,128)(2,1)}), bf16[8,4,48,1024]{3,2,1,0:T(8,128)(2,1)}, u32[]{:S(2)}, u32[]{:S(2)}) %all-to-all-start.3) | async-done | bytes 3145760 | tf_op jit(solution)/shard_map/all_to_all | solution.py:77
  387.7 8.3 %gather_fusion.4 = bf16[1024,1024]{1,0:T(8,128)(2,1)} fusion(bf16[1536,1024]{1,0:T(8,128)(2,1)} %bitcast.16, s32[1024]{0:T(1024)S(1)} %broadcast_clamp_fusion), kind=kCustom, calls=%fused_computation.4 | custom fusion | bytes 4198400 | tf_op jit(solution)/shard_map/gather | solution.py:84
  396.0 0.0 copy-start.2
  396.0 3.9 bitcast_reduce_fusion
  399.9 0.0 copy-done.2
  399.9 2.1 fusion.6
  402.0 0.0 reduce-scatter.2.cloned.1.call-done
  402.0 2.7 slice.42
  404.6 3.7 copy.53
  408.4 2.1 slice.43
  410.5 2.2 copy.54
  (11 shorter events, 0.1 us)
Async XLA Ops:
  7.2 200.5 %copy-start = (bf16[1024,4,384]{2,1,0:T(4,128)(2,1)S(1)}, bf16[1024,4,384]{2,1,0:T(4,128)(2,1)}, u32[]{:S(2)}) copy-start(bf16[1024,4,384]{2,1,0:T(4,128)(2,1)} %param.11) | copy-start | bytes 9437188
  24.1 10.4 %copy-start.1 = (bf16[128,1024]{1,0:T(8,128)(2,1)S(1)}, bf16[128,1024]{1,0:T(8,128)(2,1)}, u32[]{:S(2)}) copy-start(bf16[128,1024]{1,0:T(8,128)(2,1)} %param.9) | copy-start | bytes 786436
  131.7 76.0 %all-to-all-start.2 = ((bf16[8,4,48,1024]{3,2,1,0:T(8,128)(2,1)}), bf16[8,4,48,1024]{3,2,1,0:T(8,128)(2,1)}, u32[]{:S(2)}, u32[]{:S(2)}) async-start(bf16[8,4,48,1024]{3,2,1,0:T(8,128)(2,1)} %get-tuple-element.21), calls=%async_computation.2 | async-start | bytes 6291456 | tf_op jit(solution)/shard_map/all_to_all | solution.py:71
  136.1 265.8 %reduce-scatter.2.cloned.1.call-start = ((), (), s32[]{:S(2)}) async-start(), calls=%async_computation.5 | async-start | bytes 11796480 | tf_op jit(solution)/shard_map/reduce_scatter | solution.py:94
  213.5 5.1 %copy-start.4 = (bf16[8,4,48,384]{3,2,0,1:T(8,128)(2,1)}, bf16[8,4,48,384]{3,2,0,1:T(8,128)(2,1)S(1)}, u32[]{:S(2)}) copy-start(bf16[8,4,48,384]{3,2,0,1:T(8,128)(2,1)S(1)} %get-tuple-element.18) | copy-start | bytes 3538948
  213.5 5.1 %copy-start.5 = (bf16[8,4,48,384]{3,2,0,1:T(8,128)(2,1)}, bf16[8,4,48,384]{3,2,0,1:T(8,128)(2,1)S(1)}, u32[]{:S(2)}) copy-start(bf16[8,4,48,384]{3,2,0,1:T(8,128)(2,1)S(1)} %get-tuple-element.16) | copy-start | bytes 3538948
  213.5 5.1 %copy-start.6 = (bf16[8,4,48,384]{3,2,0,1:T(8,128)(2,1)}, bf16[8,4,48,384]{3,2,0,1:T(8,128)(2,1)S(1)}, u32[]{:S(2)}) copy-start(bf16[8,4,48,384]{3,2,0,1:T(8,128)(2,1)S(1)} %get-tuple-element.17) | copy-start | bytes 3538948
  213.6 5.1 %copy-start.3 = (bf16[8,4,48,1024]{3,2,1,0:T(8,128)(2,1)S(1)}, bf16[8,4,48,1024]{3,2,1,0:T(8,128)(2,1)}, u32[]{:S(2)}) copy-start(bf16[8,4,48,1024]{3,2,1,0:T(8,128)(2,1)} %all_to_all.20) | copy-start | bytes 9437188
  235.8 76.0 %all-to-all-start.1 = ((bf16[8,4,48,1024]{3,2,1,0:T(8,128)(2,1)}), bf16[8,4,48,1024]{3,2,1,0:T(8,128)(2,1)}, u32[]{:S(2)}, u32[]{:S(2)}) async-start(bf16[8,4,48,1024]{3,2,1,0:T(8,128)(2,1)} %copy.44), calls=%async_computation.1 | async-start | bytes 6291456 | tf_op jit(solution)/shard_map/all_to_all | solution.py:76
  311.7 76.0 %all-to-all-start.3 = ((bf16[8,4,48,1024]{3,2,1,0:T(8,128)(2,1)}), bf16[8,4,48,1024]{3,2,1,0:T(8,128)(2,1)}, u32[]{:S(2)}, u32[]{:S(2)}) async-start(bf16[8,4,48,1024]{3,2,1,0:T(8,128)(2,1)} %copy.50), calls=%async_computation.3 | async-start | bytes 6291456 | tf_op jit(solution)/shard_map/all_to_all | solution.py:77
  396.0 3.9 copy-start.2
Sparse Core Ops, SparseCore 0:
  230.7 93.8 reduce-scatter.1
where the time goes:
time: 420 us; the launch traced here: 419 us
  waiting for transfers between devices  189 us (45%)
  blocking collectives  77.7 us (18%)
  local copies, waits for them, and re-layouts  63.1 us (15%)
  matrix products  32.7 us (8%)
  other arithmetic  29 us (7%)
  between operations  14.3 us (3%)
  starting transfers between devices  13.8 us (3%)
    all_to_all x1, blocking collectives, per_device(): lax.all_to_all(x_slots, 'expert', split_axis=0, concat_axis=0, tiled=True)  77.7 us
    all_to_all x1, waiting for transfers between devices, per_device(): lax.all_to_all(grads_local, 'expert', split_axis=0, concat_axis=0, tiled=...  63.2 us
    all_to_all x1, waiting for transfers between devices, per_device(): lax.all_to_all(out_local, 'expert', split_axis=0, concat_axis=0, tiled=True)  62.9 us
    all_to_all x1, waiting for transfers between devices, per_device(): lax.all_to_all(cot_slots, 'expert', split_axis=0, concat_axis=0, tiled=True)  62.8 us
    another operation x2, other arithmetic  9.04 us
    gather x1, local copies, waits for them, and re-layouts, per_device(): tokens[token_of]  8.77 us
    dot_general x1, matrix products, forward_local(): jnp.einsum('slmd,dlf->slmf', received, w_gate_up, preferred_element_type=...  8.51 us
  transfers between devices with their start and end apart: 4, of which 3 were waited for; matrix products, arithmetic and copies ran while one was open for 11% of the time, Pallas kernels for 0%

commit v1 on v0

v1 whole, which is shorter than its diff:
```python
import jax
import jax.numpy as jnp
from jax import lax
from jax.experimental import pallas as pl
from jax.experimental.pallas import tpu as pltpu
from jax.sharding import PartitionSpec as P

CORES = 2
BF = jnp.bfloat16
F32 = jnp.float32
VMEM = 56 * 1024 * 1024


def dot(a, b):
    return lax.dot_general(a, b, (((1,), (0,)), ((), ())), preferred_element_type=F32)


def dot_t(a, b):
    return lax.dot_general(a, b, (((1,), (1,)), ((), ())), preferred_element_type=F32)


def from_further(k, peers):
    chips = peers // CORES
    return [(((z + k) % chips) * CORES + c, z * CORES + c) for z in range(chips) for c in range(CORES)]


def to_further(k, peers):
    return [(dst, src) for src, dst in from_further(k, peers)]


def partner(peers):
    return [(i, i ^ 1) for i in range(peers)]


def gather_slots(x, peers):
    chips = peers // CORES
    own = [x] + [lax.ppermute(x, "expert", from_further(k, peers)) for k in range(1, chips)]
    own = jnp.stack(own)
    other = lax.ppermute(own, "expert", partner(peers))
    return jnp.concatenate([own, other], axis=0)


def scatter_slots(own, other, peers, gate=None):
    chips = peers // CORES
    rows = own.shape[0] // chips
    got = lax.ppermute(other, "expert", partner(peers))

    def part(k):
        a = lax.slice_in_dim(own, k * rows, (k + 1) * rows, axis=0).astype(F32)
        return a + lax.slice_in_dim(got, k * rows, (k + 1) * rows, axis=0).astype(F32)

    total = part(0)
    arrived = [lax.ppermute(part(k).astype(BF), "expert", to_further(k, peers)) for k in range(1, chips)]
    for piece in arrived:
        total = total + piece.astype(F32)
    return total.astype(BF)


def transpose(x):
    rows, width = x.shape
    step = min(256, width)

    def kern(x_ref, o_ref):
        o_ref[...] = x_ref[...].T

    return pl.pallas_call(
        kern,
        grid=(width // step,),
        in_specs=[pl.BlockSpec((rows, step), lambda i: (0, i))],
        out_specs=pl.BlockSpec((step, rows), lambda i: (i, 0)),
        out_shape=jax.ShapeDtypeStruct((width, rows), x.dtype),
        compiler_params=pltpu.CompilerParams(vmem_limit_bytes=VMEM),
        name="turn",
    )(x)


def gate_column(gates, e):
    lane = lax.broadcasted_iota(jnp.int32, gates.shape, 1)
    return jnp.sum(jnp.where(lane == e, gates, 0.0), axis=1, keepdims=True)


def forward(x, gates, w_gu, w_dn):
    rows, width = x.shape
    exp_dev, _, hid = w_dn.shape
    tile = min(256, rows)
    steps = rows // tile

    def kern(x_ref, g_ref, wgu_ref, wdn_ref, fac_ref, own_ref, other_ref, acc_ref):
        e, i = pl.program_id(0), pl.program_id(1)
        proj = dot(x_ref[...], wgu_ref[0])
        gate = gate_column(g_ref[...], e)
        g, u = proj[:, :hid], proj[:, hid:]
        s = jax.nn.sigmoid(g)
        gs = g * s
        gh = (gate * (gs * u)).astype(BF)
        fac_ref[0, :, :hid] = (gate * (u * s * (1.0 + g * (1.0 - s)))).astype(BF)
        fac_ref[0, :, hid : 2 * hid] = (gate * gs).astype(BF)
        fac_ref[0, :, 2 * hid :] = gh
        out = dot_t(gh, wdn_ref[0])
        here = pl.ds(i * tile, tile)

        @pl.when(e == 0)
        def _():
            acc_ref[here, :] = out

        @pl.when(e > 0)
        def _():
            acc_ref[here, :] = acc_ref[here, :] + out

        @pl.when((e == exp_dev - 1) & (i < steps // 2))
        def _():
            own_ref[here, :] = acc_ref[here, :].astype(BF)

        @pl.when((e == exp_dev - 1) & (i >= steps // 2))
        def _():
            other_ref[pl.ds((i - steps // 2) * tile, tile), :] = acc_ref[here, :].astype(BF)

    half = jax.ShapeDtypeStruct((rows // 2, width), BF)
    return pl.pallas_call(
        kern,
        grid=(exp_dev, steps),
        in_specs=[
            pl.BlockSpec((tile, width), lambda e, i: (i, 0)),
            pl.BlockSpec((tile, exp_dev), lambda e, i: (i, 0)),
            pl.BlockSpec((1, width, 2 * hid), lambda e, i: (e, 0, 0)),
            pl.BlockSpec((1, width, hid), lambda e, i: (e, 0, 0)),
        ],
        out_specs=[
            pl.BlockSpec((1, tile, 3 * hid), lambda e, i: (e, i, 0)),
            pl.BlockSpec((rows // 2, width), lambda e, i: (0, 0)),
            pl.BlockSpec((rows // 2, width), lambda e, i: (0, 0)),
        ],
        out_shape=[jax.ShapeDtypeStruct((exp_dev, rows, 3 * hid), BF), half, half],
        scratch_shapes=[pltpu.VMEM((rows, width), F32)],
        compiler_params=pltpu.CompilerParams(vmem_limit_bytes=VMEM),
        name="forward",
    )(x, gates, w_gu, w_dn)


def weight_grads(e, blocks, sub, c, w_dn, fac, xt, ct):
    rows, width = c.shape
    hid = w_dn.shape[2]
    quarter = width // 4
    small = quarter // sub
    tile = min(256, rows)
    steps = rows // tile

    def kern(b_ref, c_ref, wdn_ref, fac_ref, gh_ref, *rest):
        xts, cts = rest[:sub], rest[sub : 2 * sub]
        outs, dp_out, dp_ref = rest[2 * sub : 2 * sub + 4], rest[2 * sub + 4], rest[2 * sub + 5]
        i = pl.program_id(0)

        @pl.when(i < steps)
        def _():
            dh = dot(c_ref[...], wdn_ref[0])
            here = pl.ds(i * tile, tile)
            d_gate = (dh * fac_ref[0, :, :hid].astype(F32)).astype(BF)
            d_up = (dh * fac_ref[0, :, hid:].astype(F32)).astype(BF)
            dp_ref[here, :hid] = d_gate
            dp_ref[here, hid:] = d_up
            dp_out[:, :hid] = d_gate
            dp_out[:, hid:] = d_up

        for q in range(4):

            @pl.when(i == steps + q)
            def _():
                lhs = jnp.concatenate([r[...] for r in xts], axis=0)
                outs[q][:, : 2 * hid] = dot(lhs, dp_ref[...]).astype(BF)
                lhs = jnp.concatenate([r[...] for r in cts], axis=0)
                outs[q][:, 2 * hid :] = dot(lhs, gh_ref[0]).astype(BF)

    def row(i, b):
        return jnp.minimum(i, steps - 1)

    def turned(k):
        return pl.BlockSpec((small, rows), lambda i, b: (b[jnp.maximum(i - steps, 0) * sub + k], 0))

    piece = jax.ShapeDtypeStruct((quarter, 3 * hid), BF)
    return pl.pallas_call(
        kern,
        grid_spec=pltpu.PrefetchScalarGridSpec(
            num_scalar_prefetch=1,
            grid=(steps + 4,),
            in_specs=[
                pl.BlockSpec((tile, width), lambda i, b: (row(i, b), 0)),
                pl.BlockSpec((1, width, hid), lambda i, b: (e, 0, 0)),
                pl.BlockSpec((1, tile, 2 * hid), lambda i, b: (e, row(i, b), 0)),
                pl.BlockSpec((1, rows, hid), lambda i, b: (e, 0, 2)),
            ]
            + [turned(k) for k in range(sub)] * 2,
            out_specs=[pl.BlockSpec((quarter, 3 * hid), lambda i, b: (0, 0))] * 4
            + [pl.BlockSpec((tile, 2 * hid), lambda i, b: (row(i, b), 0))],
            scratch_shapes=[pltpu.VMEM((rows, 2 * hid), BF)],
        ),
        out_shape=[piece] * 4 + [jax.ShapeDtypeStruct((rows, 2 * hid), BF)],
        compiler_params=pltpu.CompilerParams(vmem_limit_bytes=VMEM),
        name=f"weight_grads_{e}",
    )(blocks, c, w_dn, fac, fac, *([xt] * sub), *([ct] * sub))


def token_grads(d_proj, w_gu):
    exp_dev = len(d_proj)
    rows, wide = d_proj[0].shape
    width = w_gu.shape[1]
    tile = min(256, rows)
    steps = rows // tile

    def kern(*refs):
        dps, w_ref, own_ref, other_ref = refs[:exp_dev], refs[exp_dev], refs[exp_dev + 1], refs[exp_dev + 2]
        i = pl.program_id(0)
        acc = dot_t(dps[0][...], w_ref[0])
        for e in range(1, exp_dev):
            acc = acc + dot_t(dps[e][...], w_ref[e])

        @pl.when(i < steps // 2)
        def _():
            own_ref[...] = acc.astype(BF)

        @pl.when(i >= steps // 2)
        def _():
            other_ref[...] = acc.astype(BF)

    half = jax.ShapeDtypeStruct((rows // 2, width), BF)
    return pl.pallas_call(
        kern,
        grid=(steps,),
        in_specs=[pl.BlockSpec((tile, wide), lambda i: (i, 0))] * exp_dev
        + [pl.BlockSpec((exp_dev, width, wide), lambda i: (0, 0, 0), pipeline_mode=pl.Buffered(1))],
        out_specs=[
            pl.BlockSpec((tile, width), lambda i: (jnp.minimum(i, steps // 2 - 1), 0)),
            pl.BlockSpec((tile, width), lambda i: (jnp.maximum(i - steps // 2, 0), 0)),
        ],
        out_shape=[half, half],
        compiler_params=pltpu.CompilerParams(vmem_limit_bytes=VMEM),
        name="token_grads",
    )(*d_proj, w_gu)


def reduce_groups(keep, send, bits, groups):
    for n, bit in enumerate(bits):
        got = lax.ppermute(send, "dp", [(i, i ^ (1 << bit)) for i in range(groups)])
        total = keep.astype(F32) + got.astype(F32)
        if n == len(bits) - 1:
            return total.astype(BF)
        half = keep.shape[0] // 2
        keep, send = total[:half].astype(BF), total[half:].astype(BF)


def per_device(tokens, routes, gate_weights, cotangent, w_gate_up, w_down):
    tok_dev, active = routes.shape
    width = tokens.shape[1]
    exp_dev = w_down.shape[1]
    hid = w_down.shape[2]
    peers = lax.axis_size("expert")
    groups = lax.axis_size("dp")
    rows = tok_dev * peers
    n_bits = groups.bit_length() - 1
    orders = (tuple(range(n_bits)), tuple(reversed(range(n_bits))))

    x = gather_slots(tokens, peers).reshape(rows, width)
    small = jnp.concatenate([routes.T.astype(F32), gate_weights.T], axis=0)
    small = gather_slots(small, peers)
    c = gather_slots(cotangent, peers).reshape(rows, width)

    first = lax.axis_index("expert") * exp_dev
    named = small[:, :active, :].astype(jnp.int32)
    mine = first + jnp.arange(exp_dev, dtype=jnp.int32)
    hit = named[:, :, :, None] == mine
    gates = jnp.sum(jnp.where(hit, small[:, active:, :, None], 0.0), axis=1).reshape(rows, exp_dev)

    w_gu = jnp.transpose(w_gate_up, (1, 0, 2))
    w_dn = jnp.transpose(w_down, (1, 0, 2))

    me = lax.axis_index("dp")
    sub = max(1, groups // 2)
    blocks = []
    for want in (1, 0):
        for colour, order in enumerate(orders):
            for pos in range(groups // 2):
                full = pos + want * (groups // 2)
                rel = sum(((full >> (n_bits - 1 - n)) & 1) << bit for n, bit in enumerate(order))
                blocks.append((me ^ rel) * 2 + colour)
    blocks = jnp.stack(blocks).astype(jnp.int32)

    fac, out_own, out_other = forward(x, gates, w_gu, w_dn)
    xt = transpose(x)
    ct = transpose(c)
    d_proj, reduced = [], []
    for e in range(exp_dev):
        send_a, send_b, keep_a, keep_b, dp = weight_grads(e, blocks, sub, c, w_dn, fac, xt, ct)
        d_proj.append(dp)
        part_a = reduce_groups(keep_a, send_a, orders[0], groups)
        part_b = reduce_groups(keep_b, send_b, orders[1], groups)
        reduced.append(jnp.concatenate([part_a, part_b], axis=0))
    grad_own, grad_other = token_grads(d_proj, w_gu)
    layer_out = scatter_slots(out_own, out_other, peers)
    grad_tokens = scatter_slots(grad_own, grad_other, peers)
    summed = jnp.stack(reduced, axis=1)
    return (layer_out, grad_tokens, summed[:, :, : 2 * hid], summed[:, :, 2 * hid :])


def solution(mesh):
    rows = P(("dp", "expert"), None)
    return jax.shard_map(
        per_device,
        mesh=mesh,
        in_specs=(rows, rows, rows, rows, P(None, "expert", None), P(None, "expert", None)),
        out_specs=(rows, rows, P("dp", "expert", None), P("dp", "expert", None)),
        check_vma=False,
    )
```

time: 420 us -> 273 us (0.65)
  waiting for transfers between devices: 189 us -> 94.4 us
  Pallas kernels: 0 us -> 94.2 us
  blocking collectives: 77.7 us -> 0 us
  local copies, waits for them, and re-layouts: 63.1 us -> 24.9 us
  starting transfers between devices: 13.8 us -> 47.3 us
  matrix products: 32.7 us -> 0 us
  other arithmetic: 29 us -> 9.26 us
  between operations: 14.3 us -> 1.2 us
    all_to_all x3 -> x0, waiting for transfers between devices: 189 us -> none  [the longest x1 63.2 us: per_device(): lax.all_to_all(grads_local, 'expert', split_axis=0, concat_axis=0, tiled=...]
    ppermute x0 -> x36, waiting for transfers between devices: none -> 94.4 us  [the longest x16 40 us: reduce_groups(): got = lax.ppermute(send, 'dp', [(i, i ^ 1 << bit) for i in range(groups)])]
    pallas_call x0 -> x8, Pallas kernels: none -> 94.2 us  [the longest x4 46.3 us: weight_grads(): pl.pallas_call(kern, grid_spec=pltpu.PrefetchScalarGridSpec(num_scalar_pr...]
    all_to_all x1 -> x0, blocking collectives: 77.7 us -> none  [per_device(): lax.all_to_all(x_slots, 'expert', split_axis=0, concat_axis=0, tiled=True)]
    ppermute x0 -> x36, starting transfers between devices: none -> 47.3 us  [the longest x16 18.4 us: reduce_groups(): got = lax.ppermute(send, 'dp', [(i, i ^ 1 << bit) for i in range(groups)])]
    gather x5 -> x0, local copies, waits for them, and re-layouts: 37.1 us -> none  [the longest x1 8.77 us: per_device(): tokens[token_of]]
    dot_general x6 -> x0, matrix products: 32.7 us -> none  [the longest x1 8.51 us: forward_local(): jnp.einsum('slmd,dlf->slmf', received, w_gate_up, preferred_element_type=...]
    unnamed x18 -> x67, local copies, waits for them, and re-layouts: 7.63 us -> 22.8 us
  transfers between devices with their start and end apart: 4 -> 36, of which waited for: 3 -> 17; matrix products, arithmetic and copies ran while one was open for 11% -> 10% of each run, Pallas kernels for 0% -> 19%
where the time goes in v1:
time: 273 us; the launch traced here: 271 us
  waiting for transfers between devices  94.4 us (35%)
  Pallas kernels  94.2 us (35%)
  starting transfers between devices  47.3 us (17%)
  local copies, waits for them, and re-layouts  24.9 us (9%)
  other arithmetic  9.26 us (3%)
    pallas_call x4, Pallas kernels, weight_grads(): pl.pallas_call(kern, grid_spec=pltpu.PrefetchScalarGridSpec(num_scalar_pr...  46.3 us
    ppermute x16, waiting for transfers between devices, reduce_groups(): got = lax.ppermute(send, 'dp', [(i, i ^ 1 << bit) for i in range(groups)])  40 us
    ppermute x9, waiting for transfers between devices, gather_slots(): lax.ppermute(x, 'expert', from_further(k, peers))  27.5 us
    pallas_call x1, Pallas kernels, forward(): pl.pallas_call(kern, grid=(exp_dev, steps), in_specs=[pl.BlockSpec((tile,...  27.4 us
    ppermute x6, waiting for transfers between devices, scatter_slots(): lax.ppermute(part(k).astype(BF), 'expert', to_further(k, peers))  25.7 us
    unnamed x67, local copies, waits for them, and re-layouts  22.8 us
    ppermute x16, starting transfers between devices, reduce_groups(): got = lax.ppermute(send, 'dp', [(i, i ^ 1 << bit) for i in range(groups)])  18.4 us
    ppermute x9, starting transfers between devices, gather_slots(): lax.ppermute(x, 'expert', from_further(k, peers))  15.2 us
  transfers between devices with their start and end apart: 36, of which 17 were waited for; matrix products, arithmetic and copies ran while one was open for 10% of the time, Pallas kernels for 19%

profile of v1, /device:TPU:0, one launch (start us, length us, event | category | flops | bytes accessed | tf_op | source)
XLA Modules:
  0.0 271.3 jit_solution(16104076448084134317)
XLA Ops:
  0.6 0.7 convert_bitcast_fusion
  2.0 4.1 %collective-permute-start.5 = (f32[16,128]{1,0:T(8,128)S(1)}, f32[16,128]{1,0:T(8,128)S(1)}, u32[]{:S(2)}, u32[]{:S(2)}) collective-permute-start(f32[16,128]{1,0:T(8,128)S(1)} %get-tuple-element.71), channel_id=1, source_target_pairs={{4,0},{5,1},{6,2},{7,3},{0,4},{1,5},{2,6},{3,7},{12,8},{13,9},{14,... | collective-permute-start | bytes 24584 | tf_op jit(solution)/shard_map/ppermute | solution.py:37
  6.1 1.3 collective-permute-start.4
  8.1 3.1 %collective-permute-start = (bf16[128,1024]{1,0:T(8,128)(2,1)}, bf16[128,1024]{1,0:T(8,128)(2,1)S(1)}, u32[]{:S(2)}, u32[]{:S(2)}) collective-permute-start(bf16[128,1024]{1,0:T(8,128)(2,1)} %param.6), channel_id=1, source_target_pairs={{2,0},{3,1},{4,2},{5,3},{6,4},{7,5},{0,6},{1,7},{10,8},{11,9},{12,... | collective-permute-start | bytes 786440 | tf_op jit(solution)/shard_map/ppermute | solution.py:37
  11.3 0.7 constant_dynamic-update-slice_fusion.9
  11.9 1.7 constant_dynamic-update-slice_fusion.4
  13.6 1.0 constant_dynamic-update-slice_fusion.14
  14.6 4.1 %copy.22 = bf16[1024,4,384]{2,0,1:T(8,128)(2,1)} copy(bf16[1024,4,384]{2,1,0:T(4,128)(2,1)} %param.11) | data formatting | bytes 6291456 | tf_op args[5]
  19.1 3.4 %copy.21 = bf16[1024,4,768]{2,0,1:T(8,128)(2,1)} copy(bf16[1024,4,768]{2,1,0:T(4,128)(2,1)S(1)} %copy-done.3) | data formatting | bytes 12582912 | tf_op args[4]
  23.7 3.3 %collective-permute-start.12 = (bf16[128,1024]{1,0:T(8,128)(2,1)S(1)}, bf16[128,1024]{1,0:T(8,128)(2,1)}, u32[]{:S(2)}, u32[]{:S(2)}) collective-permute-start(bf16[128,1024]{1,0:T(8,128)(2,1)S(1)} %copy-done.7), channel_id=1, source_target_pairs={{2,0},{3,1},{4,2},{5,3},{6,4},{7,5},{0,6},{1,7},{10,8},{11,9},{12,... | collective-permute-start | bytes 786440 | tf_op jit(solution)/shard_map/ppermute | solution.py:37
  27.1 1.2 collective-permute-done.7
  28.8 1.5 collective-permute-start.13
  30.4 1.0 copy.14
  31.4 8.4 %collective-permute-done.1 = bf16[128,1024]{1,0:T(8,128)(2,1)S(1)} collective-permute-done((bf16[128,1024]{1,0:T(8,128)(2,1)S(1)}, bf16[128,1024]{1,0:T(8,128)(2,1)S(1)}, u32[]{:S(2)}, u32[]{:S(2)}) %collective-permute-start.1) | collective-permute-done | bytes 262176 | tf_op jit(solution)/shard_map/ppermute | solution.py:37
  40.1 5.5 %collective-permute-done.14 = bf16[128,1024]{1,0:T(8,128)(2,1)} collective-permute-done((bf16[128,1024]{1,0:T(8,128)(2,1)S(1)}, bf16[128,1024]{1,0:T(8,128)(2,1)}, u32[]{:S(2)}, u32[]{:S(2)}) %collective-permute-start.14) | collective-permute-done | bytes 262176 | tf_op jit(solution)/shard_map/ppermute | solution.py:37
  45.5 13.6 %collective-permute-done.13 = bf16[128,1024]{1,0:T(8,128)(2,1)} collective-permute-done((bf16[128,1024]{1,0:T(8,128)(2,1)S(1)}, bf16[128,1024]{1,0:T(8,128)(2,1)}, u32[]{:S(2)}, u32[]{:S(2)}) %collective-permute-start.13) | collective-permute-done | bytes 262176 | tf_op jit(solution)/shard_map/ppermute | solution.py:37
  59.2 2.2 pad_maximum_fusion.2
  61.4 1.0 constant_dynamic-update-slice_fusion.3
  62.4 1.0 constant_dynamic-update-slice_fusion.2
  63.4 1.0 constant_dynamic-update-slice_fusion.13
  64.3 1.0 constant_dynamic-update-slice_fusion.12
  65.3 1.0 constant_dynamic-update-slice_fusion.11
  66.4 1.3 copy-done.2
  67.7 4.1 %turn.2.rest_0_.rest_1_ = bf16[1024,1024]{1,0:T(8,128)(2,1)} custom-call(bf16[1024,1024]{1,0:T(8,128)(2,1)} %bitcast.65), custom_call_target="tpu_custom_call" | custom-call | tf_op jit(solution)/shard_map/turn/pallas_call | solution.py:66
  71.9 1.3 copy-done
  73.2 4.1 %turn.3.rest_2_.rest_3_ = bf16[1024,1024]{1,0:T(8,128)(2,1)} custom-call(bf16[1024,1024]{1,0:T(8,128)(2,1)} %bitcast.60), custom_call_target="tpu_custom_call" | custom-call | tf_op jit(solution)/shard_map/turn/pallas_call | solution.py:66
  77.4 27.4 %forward.1 = (bf16[4,1024,1152]{2,1,0:T(8,128)(2,1)}, bf16[512,1024]{1,0:T(8,128)(2,1)}, bf16[512,1024]{1,0:T(8,128)(2,1)}) custom-call(bf16[1024,1024]{1,0:T(8,128)(2,1)} %bitcast.66, f32[1024,4]{1,0:T(8,128)} %bitcast.67, bf16[4,1024,768]{2,1,0:T(8,128)(2,1)} %bitcast.58, bf16[4,1024,384]{2,1,0:T(8,128)(2,1)} %bitcast.53), custom_call_target="tpu_custom_call" | custom-call | tf_op jit(solution)/shard_map/forward/pallas_call | solution.py:119
  104.7 11.5 %weight_grads_3.1 = (bf16[256,1152]{1,0:T(8,128)(2,1)}, bf16[256,1152]{1,0:T(8,128)(2,1)}, bf16[256,1152]{1,0:T(8,128)(2,1)}, bf16[256,1152]{1,0:T(8,128)(2,1)}, bf16[1024,768]{1,0:T(8,128)(2,1)}) custom-call(s32[8]{0:T(128)} %stack.105.b_ref, bf16[1024,1024]{1,0:T(8,128)(2,1)} %bitcast.61, bf16[4,1024,384]{2,1,0:T(8,128)(2,1)} %bitcast.54, ...), custom_call_target="tpu_custom_call" | custom-call | tf_op jit(solution)/shard_map/weight_grads_3/pallas_call | solution.py:180
  116.2 1.5 collective-permute-start.32
  117.7 1.5 collective-permute-start.34
  119.2 11.5 %weight_grads_2.1 = (bf16[256,1152]{1,0:T(8,128)(2,1)}, bf16[256,1152]{1,0:T(8,128)(2,1)}, bf16[256,1152]{1,0:T(8,128)(2,1)}, bf16[256,1152]{1,0:T(8,128)(2,1)}, bf16[1024,768]{1,0:T(8,128)(2,1)}) custom-call(s32[8]{0:T(128)} %stack.105.b_ref, bf16[1024,1024]{1,0:T(8,128)(2,1)} %bitcast.62, bf16[4,1024,384]{2,1,0:T(8,128)(2,1)} %bitcast.55, ...), custom_call_target="tpu_custom_call" | custom-call | tf_op jit(solution)/shard_map/weight_grads_2/pallas_call | solution.py:180
  130.7 11.5 %weight_grads_1.1 = (bf16[256,1152]{1,0:T(8,128)(2,1)}, bf16[256,1152]{1,0:T(8,128)(2,1)}, bf16[256,1152]{1,0:T(8,128)(2,1)}, bf16[256,1152]{1,0:T(8,128)(2,1)}, bf16[1024,768]{1,0:T(8,128)(2,1)}) custom-call(s32[8]{0:T(128)} %stack.105.b_ref, bf16[1024,1024]{1,0:T(8,128)(2,1)} %bitcast.63, bf16[4,1024,384]{2,1,0:T(8,128)(2,1)} %bitcast.56, ...), custom_call_target="tpu_custom_call" | custom-call | tf_op jit(solution)/shard_map/weight_grads_1/pallas_call | solution.py:180
  142.2 11.8 %weight_grads_0.1 = (bf16[256,1152]{1,0:T(8,128)(2,1)}, bf16[256,1152]{1,0:T(8,128)(2,1)}, bf16[256,1152]{1,0:T(8,128)(2,1)}, bf16[256,1152]{1,0:T(8,128)(2,1)}, bf16[1024,768]{1,0:T(8,128)(2,1)}) custom-call(s32[8]{0:T(128)} %stack.105.b_ref, bf16[1024,1024]{1,0:T(8,128)(2,1)} %bitcast.64, bf16[4,1024,384]{2,1,0:T(8,128)(2,1)} %bitcast.57, ...), custom_call_target="tpu_custom_call" | custom-call | tf_op jit(solution)/shard_map/weight_grads_0/pallas_call | solution.py:180
  155.3 12.2 %token_grads.1 = (bf16[512,1024]{1,0:T(8,128)(2,1)}, bf16[512,1024]{1,0:T(8,128)(2,1)}) custom-call(bf16[1024,768]{1,0:T(8,128)(2,1)} %get-tuple-element.32.refs_0_, bf16[1024,768]{1,0:T(8,128)(2,1)} %get-tuple-element.33.refs_1_, bf16[1024,768]{1,0:T(8,128)(2,1)} %get-tuple-element.34.refs_2_, bf16[1024,768]{1,0:T(8,128)(2,1)} %get-tuple-element.35.refs_3_, ...), custom_call_target="tpu_custom_call" | custom-call | tf_op jit(solution)/shard_map/token_grads/pallas_call | solution.py:225
  167.6 1.6 collective-permute-start.24
  169.3 1.5 collective-permute-start.26
  171.0 0.8 collective-permute-start.20
  172.8 11.1 %collective-permute-done.24 = bf16[256,1152]{1,0:T(8,128)(2,1)S(1)} collective-permute-done((bf16[256,1152]{1,0:T(8,128)(2,1)S(1)}, bf16[256,1152]{1,0:T(8,128)(2,1)S(1)}, u32[]{:S(2)}, u32[]{:S(2)}) %collective-permute-start.24) | collective-permute-done | bytes 589856 | tf_op jit(solution)/shard_map/ppermute | solution.py:242
  184.1 1.5 collective-permute-done.26
  185.6 1.5 collective-permute-start.33
  187.4 8.0 %collective-permute-done.20 = bf16[256,1152]{1,0:T(8,128)(2,1)S(1)} collective-permute-done((bf16[256,1152]{1,0:T(8,128)(2,1)S(1)}, bf16[256,1152]{1,0:T(8,128)(2,1)S(1)}, u32[]{:S(2)}, u32[]{:S(2)}) %collective-permute-start.20) | collective-permute-done | bytes 589856 | tf_op jit(solution)/shard_map/ppermute | solution.py:242
  195.4 1.5 collective-permute-start.35
  197.1 1.2 collective-permute-done.22
  198.2 1.5 collective-permute-start.29
  199.9 4.7 %collective-permute-done.33 = bf16[128,1152]{1,0:T(8,128)(2,1)S(1)} collective-permute-done((bf16[128,1152]{1,0:T(8,128)(2,1)S(1)}, bf16[128,1152]{1,0:T(8,128)(2,1)S(1)}, u32[]{:S(2)}, u32[]{:S(2)}) %collective-permute-start.33) | collective-permute-done | bytes 294944 | tf_op jit(solution)/shard_map/ppermute | solution.py:242
  204.5 0.7 collective-permute-start.31
  205.4 1.5 collective-permute-start.25
  207.0 3.9 %collective-permute-done.29 = bf16[128,1152]{1,0:T(8,128)(2,1)S(1)} collective-permute-done((bf16[128,1152]{1,0:T(8,128)(2,1)S(1)}, bf16[128,1152]{1,0:T(8,128)(2,1)S(1)}, u32[]{:S(2)}, u32[]{:S(2)}) %collective-permute-start.29) | collective-permute-done | bytes 294944 | tf_op jit(solution)/shard_map/ppermute | solution.py:242
  210.9 0.7 collective-permute-start.27
  211.7 1.5 collective-permute-start.21
  213.3 3.9 %collective-permute-done.25 = bf16[128,1152]{1,0:T(8,128)(2,1)S(1)} collective-permute-done((bf16[128,1152]{1,0:T(8,128)(2,1)S(1)}, bf16[128,1152]{1,0:T(8,128)(2,1)S(1)}, u32[]{:S(2)}, u32[]{:S(2)}) %collective-permute-start.25) | collective-permute-done | bytes 294944 | tf_op jit(solution)/shard_map/ppermute | solution.py:242
  217.2 0.7 collective-permute-start.23
  218.1 4.0 %collective-permute-done.21 = bf16[128,1152]{1,0:T(8,128)(2,1)S(1)} collective-permute-done((bf16[128,1152]{1,0:T(8,128)(2,1)S(1)}, bf16[128,1152]{1,0:T(8,128)(2,1)S(1)}, u32[]{:S(2)}, u32[]{:S(2)}) %collective-permute-start.21) | collective-permute-done | bytes 294944 | tf_op jit(solution)/shard_map/ppermute | solution.py:242
  222.2 1.7 collective-permute-done.23
  224.5 0.8 copy-done.4
  225.7 3.8 %collective-permute-start.11 = (bf16[128,1024]{1,0:T(8,128)(2,1)S(1)}, bf16[128,1024]{1,0:T(8,128)(2,1)S(1)}, u32[]{:S(2)}, u32[]{:S(2)}) collective-permute-start(bf16[128,1024]{1,0:T(8,128)(2,1)S(1)} %get-tuple-element.66), channel_id=1, source_target_pairs={{0,6},{1,7},{2,0},{3,1},{4,2},{5,3},{6,4},{7,5},{8,14},{9,15},{10,... | collective-permute-start | bytes 786440 | tf_op jit(solution)/shard_map/ppermute | solution.py:53
  229.7 2.4 copy.17
  232.1 1.5 copy.18
  234.5 3.3 %collective-permute-start.19 = (bf16[128,1024]{1,0:T(8,128)(2,1)S(1)}, bf16[128,1024]{1,0:T(8,128)(2,1)S(1)}, u32[]{:S(2)}, u32[]{:S(2)}) collective-permute-start(bf16[128,1024]{1,0:T(8,128)(2,1)S(1)} %get-tuple-element.63), channel_id=1, source_target_pairs={{0,6},{1,7},{2,0},{3,1},{4,2},{5,3},{6,4},{7,5},{8,14},{9,15},{10,... | collective-permute-start | bytes 786440 | tf_op jit(solution)/shard_map/ppermute | solution.py:53
  237.8 5.9 %collective-permute-start.18 = (bf16[128,1024]{1,0:T(8,128)(2,1)S(1)}, bf16[128,1024]{1,0:T(8,128)(2,1)S(1)}, u32[]{:S(2)}, u32[]{:S(2)}) collective-permute-start(bf16[128,1024]{1,0:T(8,128)(2,1)S(1)} %get-tuple-element.64), channel_id=1, source_target_pairs={{0,4},{1,5},{2,6},{3,7},{4,0},{5,1},{6,2},{7,3},{8,12},{9,13},{10,... | collective-permute-start | bytes 786440 | tf_op jit(solution)/shard_map/ppermute | solution.py:53
  243.7 14.5 %collective-permute-done.10 = bf16[128,1024]{1,0:T(8,128)(2,1)S(1)} collective-permute-done((bf16[128,1024]{1,0:T(8,128)(2,1)S(1)}, bf16[128,1024]{1,0:T(8,128)(2,1)S(1)}, u32[]{:S(2)}, u32[]{:S(2)}) %collective-permute-start.10) | collective-permute-done | bytes 262176 | tf_op jit(solution)/shard_map/ppermute | solution.py:53
  258.2 0.9 add_convert_fusion.20
  259.1 11.2 %collective-permute-done.18 = bf16[128,1024]{1,0:T(8,128)(2,1)S(1)} collective-permute-done((bf16[128,1024]{1,0:T(8,128)(2,1)S(1)}, bf16[128,1024]{1,0:T(8,128)(2,1)S(1)}, u32[]{:S(2)}, u32[]{:S(2)}) %collective-permute-start.18) | collective-permute-done | bytes 262176 | tf_op jit(solution)/shard_map/ppermute | solution.py:53
  270.3 0.9 add_convert_fusion.16
  (132 shorter events, 10.0 us)
Async XLA Ops:
  2.0 21.1 %collective-permute-start.5 = (f32[16,128]{1,0:T(8,128)S(1)}, f32[16,128]{1,0:T(8,128)S(1)}, u32[]{:S(2)}, u32[]{:S(2)}) collective-permute-start(f32[16,128]{1,0:T(8,128)S(1)} %get-tuple-element.71), channel_id=1, source_target_pairs={{4,0},{5,1},{6,2},{7,3},{0,4},{1,5},{2,6},{3,7},{12,8},{13,9},{14,... | collective-permute-start | bytes 24584 | tf_op jit(solution)/shard_map/ppermute | solution.py:37
  6.1 17.6 %collective-permute-start.4 = (f32[16,128]{1,0:T(8,128)S(1)}, f32[16,128]{1,0:T(8,128)S(1)}, u32[]{:S(2)}, u32[]{:S(2)}) collective-permute-start(f32[16,128]{1,0:T(8,128)S(1)} %get-tuple-element.71), channel_id=1, source_target_pairs={{2,0},{3,1},{4,2},{5,3},{6,4},{7,5},{0,6},{1,7},{10,8},{11,9},{12,... | collective-permute-start | bytes 24584 | tf_op jit(solution)/shard_map/ppermute | solution.py:37
  7.4 19.6 %collective-permute-start.6 = (f32[16,128]{1,0:T(8,128)S(1)}, f32[16,128]{1,0:T(8,128)S(1)}, u32[]{:S(2)}, u32[]{:S(2)}) collective-permute-start(f32[16,128]{1,0:T(8,128)S(1)} %get-tuple-element.71), channel_id=1, source_target_pairs={{6,0},{7,1},{0,2},{1,3},{2,4},{3,5},{4,6},{5,7},{14,8},{15,9},{8,1... | collective-permute-start | bytes 24584 | tf_op jit(solution)/shard_map/ppermute | solution.py:37
  8.1 20.7 %collective-permute-start = (bf16[128,1024]{1,0:T(8,128)(2,1)}, bf16[128,1024]{1,0:T(8,128)(2,1)S(1)}, u32[]{:S(2)}, u32[]{:S(2)}) collective-permute-start(bf16[128,1024]{1,0:T(8,128)(2,1)} %param.6), channel_id=1, source_target_pairs={{2,0},{3,1},{4,2},{5,3},{6,4},{7,5},{0,6},{1,7},{10,8},{11,9},{12,... | collective-permute-start | bytes 786440 | tf_op jit(solution)/shard_map/ppermute | solution.py:37
  11.2 20.2 %collective-permute-start.2 = (bf16[128,1024]{1,0:T(8,128)(2,1)}, bf16[128,1024]{1,0:T(8,128)(2,1)S(1)}, u32[]{:S(2)}, u32[]{:S(2)}) collective-permute-start(bf16[128,1024]{1,0:T(8,128)(2,1)} %param.6), channel_id=1, source_target_pairs={{6,0},{7,1},{0,2},{1,3},{2,4},{3,5},{4,6},{5,7},{14,8},{15,9},{8,1... | collective-permute-start | bytes 786440 | tf_op jit(solution)/shard_map/ppermute | solution.py:37
  14.6 4.5 %copy-start.3 = (bf16[1024,4,768]{2,1,0:T(4,128)(2,1)S(1)}, bf16[1024,4,768]{2,1,0:T(4,128)(2,1)}, u32[]{:S(2)}) copy-start(bf16[1024,4,768]{2,1,0:T(4,128)(2,1)} %param.10) | copy-start | bytes 18874372
  19.1 4.1 %copy-start.6 = (bf16[128,1024]{1,0:T(8,128)(2,1)S(1)}, bf16[128,1024]{1,0:T(8,128)(2,1)}, u32[]{:S(2)}) copy-start(bf16[128,1024]{1,0:T(8,128)(2,1)} %param.6) | copy-start | bytes 786436
  19.1 4.6 %copy-start.7 = (bf16[128,1024]{1,0:T(8,128)(2,1)S(1)}, bf16[128,1024]{1,0:T(8,128)(2,1)}, u32[]{:S(2)}) copy-start(bf16[128,1024]{1,0:T(8,128)(2,1)} %param.9) | copy-start | bytes 786436
  23.1 16.7 %collective-permute-start.1 = (bf16[128,1024]{1,0:T(8,128)(2,1)S(1)}, bf16[128,1024]{1,0:T(8,128)(2,1)S(1)}, u32[]{:S(2)}, u32[]{:S(2)}) collective-permute-start(bf16[128,1024]{1,0:T(8,128)(2,1)S(1)} %copy-done.6), channel_id=1, source_target_pairs={{4,0},{5,1},{6,2},{7,3},{0,4},{1,5},{2,6},{3,7},{12,8},{13,9},{14,... | collective-permute-start | bytes 786440 | tf_op jit(solution)/shard_map/ppermute | solution.py:37
  23.7 16.4 %collective-permute-start.12 = (bf16[128,1024]{1,0:T(8,128)(2,1)S(1)}, bf16[128,1024]{1,0:T(8,128)(2,1)}, u32[]{:S(2)}, u32[]{:S(2)}) collective-permute-start(bf16[128,1024]{1,0:T(8,128)(2,1)S(1)} %copy-done.7), channel_id=1, source_target_pairs={{2,0},{3,1},{4,2},{5,3},{6,4},{7,5},{0,6},{1,7},{10,8},{11,9},{12,... | collective-permute-start | bytes 786440 | tf_op jit(solution)/shard_map/ppermute | solution.py:37
  27.0 1.2 collective-permute-start.7
  28.2 17.3 %collective-permute-start.14 = (bf16[128,1024]{1,0:T(8,128)(2,1)S(1)}, bf16[128,1024]{1,0:T(8,128)(2,1)}, u32[]{:S(2)}, u32[]{:S(2)}) collective-permute-start(bf16[128,1024]{1,0:T(8,128)(2,1)S(1)} %copy-done.7), channel_id=1, source_target_pairs={{6,0},{7,1},{0,2},{1,3},{2,4},{3,5},{4,6},{5,7},{14,8},{15,9},{8,1... | collective-permute-start | bytes 786440 | tf_op jit(solution)/shard_map/ppermute | solution.py:37
  28.8 30.4 %copy-start.8 = (bf16[128,1024]{1,0:T(8,128)(2,1)}, bf16[128,1024]{1,0:T(8,128)(2,1)S(1)}, u32[]{:S(2)}) copy-start(bf16[128,1024]{1,0:T(8,128)(2,1)S(1)} %collective-permute-done) | copy-start | bytes 786436
  28.8 30.4 %collective-permute-start.13 = (bf16[128,1024]{1,0:T(8,128)(2,1)S(1)}, bf16[128,1024]{1,0:T(8,128)(2,1)}, u32[]{:S(2)}, u32[]{:S(2)}) collective-permute-start(bf16[128,1024]{1,0:T(8,128)(2,1)S(1)} %copy-done.7), channel_id=1, source_target_pairs={{4,0},{5,1},{6,2},{7,3},{0,4},{1,5},{2,6},{3,7},{12,8},{13,9},{14,... | collective-permute-start | bytes 786440 | tf_op jit(solution)/shard_map/ppermute | solution.py:37
  39.8 19.4 %copy-start.9 = (bf16[128,1024]{1,0:T(8,128)(2,1)}, bf16[128,1024]{1,0:T(8,128)(2,1)S(1)}, u32[]{:S(2)}) copy-start(bf16[128,1024]{1,0:T(8,128)(2,1)S(1)} %collective-permute-done.1) | copy-start | bytes 786436
  40.0 21.4 %copy-start.1 = (bf16[8,128,1024]{2,1,0:T(8,128)(2,1)S(1)}, bf16[8,128,1024]{2,1,0:T(8,128)(2,1)}, u32[]{:S(2)}) copy-start(bf16[8,128,1024]{2,1,0:T(8,128)(2,1)} %constant_dynamic-update-slice_fusion.4) | copy-start | bytes 6291460
  40.0 26.3 %collective-permute-start.3 = (bf16[4,128,1024]{2,1,0:T(8,128)(2,1)S(1)}, bf16[4,128,1024]{2,1,0:T(8,128)(2,1)S(1)}, u32[]{:S(2)}, u32[]{:S(2)}) collective-permute-start(bf16[4,128,1024]{2,1,0:T(8,128)(2,1)S(1)} %pad_maximum_fusion.1), channel_id=1, source_target_pairs={{0,1},{1,0},{2,3},{3,2},{4,5},{5,4},{6,7},{7,6},{8,9},{9,8},{10,11... | collective-permute-start | bytes 3145736 | tf_op jit(solution)/shard_map/ppermute | solution.py:39
  61.4 10.4 %collective-permute-start.15 = (bf16[4,128,1024]{2,1,0:T(8,128)(2,1)}, bf16[4,128,1024]{2,1,0:T(8,128)(2,1)S(1)}, u32[]{:S(2)}, u32[]{:S(2)}) collective-permute-start(bf16[4,128,1024]{2,1,0:T(8,128)(2,1)} %pad_maximum_fusion.2), channel_id=1, source_target_pairs={{0,1},{1,0},{2,3},{3,2},{4,5},{5,4},{6,7},{7,6},{8,9},{9,8},{10,11... | collective-permute-start | bytes 3145736 | tf_op jit(solution)/shard_map/ppermute | solution.py:39
  66.4 1.3 copy-start.2
  71.9 1.3 copy-start
  116.2 51.4 %collective-permute-start.32 = (bf16[256,1152]{1,0:T(8,128)(2,1)}, bf16[256,1152]{1,0:T(8,128)(2,1)S(1)}, u32[]{:S(2)}, u32[]{:S(2)}) collective-permute-start(bf16[256,1152]{1,0:T(8,128)(2,1)} %get-tuple-element.51), channel_id=1, source_target_pairs={{0,8},{8,0},{16,24},{24,16},{1,9},{9,1},{17,25},{25,17},{2,10},{10... | collective-permute-start | bytes 1769480 | tf_op jit(solution)/shard_map/ppermute | solution.py:242
  117.7 51.6 %collective-permute-start.34 = (bf16[256,1152]{1,0:T(8,128)(2,1)}, bf16[256,1152]{1,0:T(8,128)(2,1)S(1)}, u32[]{:S(2)}, u32[]{:S(2)}) collective-permute-start(bf16[256,1152]{1,0:T(8,128)(2,1)} %get-tuple-element.53), channel_id=1, source_target_pairs={{0,16},{8,24},{16,0},{24,8},{1,17},{9,25},{17,1},{25,9},{2,18},{10... | collective-permute-start | bytes 1769480 | tf_op jit(solution)/shard_map/ppermute | solution.py:242
  142.2 11.9 %copy-start.18 = (bf16[512,1024]{1,0:T(8,128)(2,1)S(1)}, bf16[512,1024]{1,0:T(8,128)(2,1)}, u32[]{:S(2)}) copy-start(bf16[512,1024]{1,0:T(8,128)(2,1)} %get-tuple-element.30) | copy-start | bytes 3145732
  142.2 11.9 %copy-start.25 = (bf16[256,1152]{1,0:T(8,128)(2,1)S(1)}, bf16[256,1152]{1,0:T(8,128)(2,1)}, u32[]{:S(2)}) copy-start(bf16[256,1152]{1,0:T(8,128)(2,1)} %get-tuple-element.47) | copy-start | bytes 1769476
  142.2 12.6 %copy-start.24 = (bf16[256,1152]{1,0:T(8,128)(2,1)S(1)}, bf16[256,1152]{1,0:T(8,128)(2,1)}, u32[]{:S(2)}) copy-start(bf16[256,1152]{1,0:T(8,128)(2,1)} %get-tuple-element.49) | copy-start | bytes 1769476
  154.1 70.4 %collective-permute-start.8 = (bf16[512,1024]{1,0:T(8,128)(2,1)S(1)}, bf16[512,1024]{1,0:T(8,128)(2,1)S(1)}, u32[]{:S(2)}, u32[]{:S(2)}) collective-permute-start(bf16[512,1024]{1,0:T(8,128)(2,1)S(1)} %copy-done.18), channel_id=1, source_target_pairs={{0,1},{1,0},{2,3},{3,2},{4,5},{5,4},{6,7},{7,6},{8,9},{9,8},{10,11... | collective-permute-start | bytes 3145736 | tf_op jit(solution)/shard_map/ppermute | solution.py:46
  154.2 16.8 %collective-permute-start.28 = (bf16[256,1152]{1,0:T(8,128)(2,1)S(1)}, bf16[256,1152]{1,0:T(8,128)(2,1)S(1)}, u32[]{:S(2)}, u32[]{:S(2)}) collective-permute-start(bf16[256,1152]{1,0:T(8,128)(2,1)S(1)} %copy-done.25), channel_id=1, source_target_pairs={{0,8},{8,0},{16,24},{24,16},{1,9},{9,1},{17,25},{25,17},{2,10},{10... | collective-permute-start | bytes 1769480 | tf_op jit(solution)/shard_map/ppermute | solution.py:242
  154.8 17.1 %collective-permute-start.30 = (bf16[256,1152]{1,0:T(8,128)(2,1)S(1)}, bf16[256,1152]{1,0:T(8,128)(2,1)S(1)}, u32[]{:S(2)}, u32[]{:S(2)}) collective-permute-start(bf16[256,1152]{1,0:T(8,128)(2,1)S(1)} %copy-done.24), channel_id=1, source_target_pairs={{0,16},{8,24},{16,0},{24,8},{1,17},{9,25},{17,1},{25,9},{2,18},{10... | collective-permute-start | bytes 1769480 | tf_op jit(solution)/shard_map/ppermute | solution.py:242
  155.3 12.3 %copy-start.23 = (bf16[256,1152]{1,0:T(8,128)(2,1)S(1)}, bf16[256,1152]{1,0:T(8,128)(2,1)}, u32[]{:S(2)}) copy-start(bf16[256,1152]{1,0:T(8,128)(2,1)} %get-tuple-element.43) | copy-start | bytes 1769476
  155.3 13.8 %copy-start.17 = (bf16[256,1152]{1,0:T(8,128)(2,1)S(1)}, bf16[256,1152]{1,0:T(8,128)(2,1)}, u32[]{:S(2)}) copy-start(bf16[256,1152]{1,0:T(8,128)(2,1)} %get-tuple-element.50) | copy-start | bytes 1769476
  167.6 1.7 copy-start.22
  167.6 3.3 %copy-start.15 = (bf16[256,1152]{1,0:T(8,128)(2,1)S(1)}, bf16[256,1152]{1,0:T(8,128)(2,1)}, u32[]{:S(2)}) copy-start(bf16[256,1152]{1,0:T(8,128)(2,1)} %get-tuple-element.52) | copy-start | bytes 1769476
  167.6 16.3 %collective-permute-start.24 = (bf16[256,1152]{1,0:T(8,128)(2,1)S(1)}, bf16[256,1152]{1,0:T(8,128)(2,1)S(1)}, u32[]{:S(2)}, u32[]{:S(2)}) collective-permute-start(bf16[256,1152]{1,0:T(8,128)(2,1)S(1)} %copy-done.23), channel_id=1, source_target_pairs={{0,8},{8,0},{16,24},{24,16},{1,9},{9,1},{17,25},{25,17},{2,10},{10... | collective-permute-start | bytes 1769480 | tf_op jit(solution)/shard_map/ppermute | solution.py:242
  169.2 1.9 copy-start.21
  169.2 2.7 copy-start.16
  169.3 16.3 %collective-permute-start.26 = (bf16[256,1152]{1,0:T(8,128)(2,1)S(1)}, bf16[256,1152]{1,0:T(8,128)(2,1)S(1)}, u32[]{:S(2)}, u32[]{:S(2)}) collective-permute-start(bf16[256,1152]{1,0:T(8,128)(2,1)S(1)} %copy-done.22), channel_id=1, source_target_pairs={{0,16},{8,24},{16,0},{24,8},{1,17},{9,25},{17,1},{25,9},{2,18},{10... | collective-permute-start | bytes 1769480 | tf_op jit(solution)/shard_map/ppermute | solution.py:242
  170.9 1.1 copy-start.20
  170.9 1.8 copy-start.14
  171.0 24.4 %collective-permute-start.20 = (bf16[256,1152]{1,0:T(8,128)(2,1)S(1)}, bf16[256,1152]{1,0:T(8,128)(2,1)S(1)}, u32[]{:S(2)}, u32[]{:S(2)}) collective-permute-start(bf16[256,1152]{1,0:T(8,128)(2,1)S(1)} %copy-done.21), channel_id=1, source_target_pairs={{0,8},{8,0},{16,24},{24,16},{1,9},{9,1},{17,25},{25,17},{2,10},{10... | collective-permute-start | bytes 1769480 | tf_op jit(solution)/shard_map/ppermute | solution.py:242
  171.8 12.0 %copy-start.19 = (bf16[512,1024]{1,0:T(8,128)(2,1)S(1)}, bf16[512,1024]{1,0:T(8,128)(2,1)}, u32[]{:S(2)}) copy-start(bf16[512,1024]{1,0:T(8,128)(2,1)} %get-tuple-element.37) | copy-start | bytes 3145732
  171.8 12.0 %copy-start.13 = (bf16[256,1152]{1,0:T(8,128)(2,1)S(1)}, bf16[256,1152]{1,0:T(8,128)(2,1)}, u32[]{:S(2)}) copy-start(bf16[256,1152]{1,0:T(8,128)(2,1)} %get-tuple-element.42) | copy-start | bytes 1769476
  172.0 26.2 %collective-permute-start.22 = (bf16[256,1152]{1,0:T(8,128)(2,1)S(1)}, bf16[256,1152]{1,0:T(8,128)(2,1)S(1)}, u32[]{:S(2)}, u32[]{:S(2)}) collective-permute-start(bf16[256,1152]{1,0:T(8,128)(2,1)S(1)} %copy-done.20), channel_id=1, source_target_pairs={{0,16},{8,24},{16,0},{24,8},{1,17},{9,25},{17,1},{25,9},{2,18},{10... | collective-permute-start | bytes 1769480 | tf_op jit(solution)/shard_map/ppermute | solution.py:242
  172.8 14.3 %copy-start.12 = (bf16[256,1152]{1,0:T(8,128)(2,1)S(1)}, bf16[256,1152]{1,0:T(8,128)(2,1)}, u32[]{:S(2)}) copy-start(bf16[256,1152]{1,0:T(8,128)(2,1)} %get-tuple-element.44) | copy-start | bytes 1769476
  183.9 49.7 %collective-permute-start.16 = (bf16[512,1024]{1,0:T(8,128)(2,1)S(1)}, bf16[512,1024]{1,0:T(8,128)(2,1)S(1)}, u32[]{:S(2)}, u32[]{:S(2)}) collective-permute-start(bf16[512,1024]{1,0:T(8,128)(2,1)S(1)} %copy-done.19), channel_id=1, source_target_pairs={{0,1},{1,0},{2,3},{3,2},{4,5},{5,4},{6,7},{7,6},{8,9},{9,8},{10,11... | collective-permute-start | bytes 3145736 | tf_op jit(solution)/shard_map/ppermute | solution.py:46
  185.6 19.0 %collective-permute-start.33 = (bf16[128,1152]{1,0:T(8,128)(2,1)S(1)}, bf16[128,1152]{1,0:T(8,128)(2,1)S(1)}, u32[]{:S(2)}, u32[]{:S(2)}) collective-permute-start(bf16[128,1152]{1,0:T(8,128)(2,1)S(1)} %slice.183), channel_id=1, source_target_pairs={{0,16},{8,24},{16,0},{24,8},{1,17},{9,25},{17,1},{25,9},{2,18},{10... | collective-permute-start | bytes 884744 | tf_op jit(solution)/shard_map/ppermute | solution.py:242
  187.2 9.7 %copy-start.11 = (bf16[256,1152]{1,0:T(8,128)(2,1)S(1)}, bf16[256,1152]{1,0:T(8,128)(2,1)}, u32[]{:S(2)}) copy-start(bf16[256,1152]{1,0:T(8,128)(2,1)} %get-tuple-element.38) | copy-start | bytes 1769476
  187.3 12.4 %copy-start.10 = (bf16[256,1152]{1,0:T(8,128)(2,1)S(1)}, bf16[256,1152]{1,0:T(8,128)(2,1)}, u32[]{:S(2)}) copy-start(bf16[256,1152]{1,0:T(8,128)(2,1)} %get-tuple-element.40) | copy-start | bytes 1769476
  195.4 10.0 %collective-permute-start.35 = (bf16[128,1152]{1,0:T(8,128)(2,1)S(1)}, bf16[128,1152]{1,0:T(8,128)(2,1)S(1)}, u32[]{:S(2)}, u32[]{:S(2)}) collective-permute-start(bf16[128,1152]{1,0:T(8,128)(2,1)S(1)} %slice.185), channel_id=1, source_target_pairs={{0,8},{8,0},{16,24},{24,16},{1,9},{9,1},{17,25},{25,17},{2,10},{10... | collective-permute-start | bytes 884744 | tf_op jit(solution)/shard_map/ppermute | solution.py:242
  198.2 12.6 %collective-permute-start.29 = (bf16[128,1152]{1,0:T(8,128)(2,1)S(1)}, bf16[128,1152]{1,0:T(8,128)(2,1)S(1)}, u32[]{:S(2)}, u32[]{:S(2)}) collective-permute-start(bf16[128,1152]{1,0:T(8,128)(2,1)S(1)} %slice.179), channel_id=1, source_target_pairs={{0,16},{8,24},{16,0},{24,8},{1,17},{9,25},{17,1},{25,9},{2,18},{10... | collective-permute-start | bytes 884744 | tf_op jit(solution)/shard_map/ppermute | solution.py:242
  204.5 7.2 %collective-permute-start.31 = (bf16[128,1152]{1,0:T(8,128)(2,1)S(1)}, bf16[128,1152]{1,0:T(8,128)(2,1)S(1)}, u32[]{:S(2)}, u32[]{:S(2)}) collective-permute-start(bf16[128,1152]{1,0:T(8,128)(2,1)S(1)} %slice.181), channel_id=1, source_target_pairs={{0,8},{8,0},{16,24},{24,16},{1,9},{9,1},{17,25},{25,17},{2,10},{10... | collective-permute-start | bytes 884744 | tf_op jit(solution)/shard_map/ppermute | solution.py:242
  205.4 11.8 %collective-permute-start.25 = (bf16[128,1152]{1,0:T(8,128)(2,1)S(1)}, bf16[128,1152]{1,0:T(8,128)(2,1)S(1)}, u32[]{:S(2)}, u32[]{:S(2)}) collective-permute-start(bf16[128,1152]{1,0:T(8,128)(2,1)S(1)} %slice.175), channel_id=1, source_target_pairs={{0,16},{8,24},{16,0},{24,8},{1,17},{9,25},{17,1},{25,9},{2,18},{10... | collective-permute-start | bytes 884744 | tf_op jit(solution)/shard_map/ppermute | solution.py:242
  210.9 7.2 %collective-permute-start.27 = (bf16[128,1152]{1,0:T(8,128)(2,1)S(1)}, bf16[128,1152]{1,0:T(8,128)(2,1)S(1)}, u32[]{:S(2)}, u32[]{:S(2)}) collective-permute-start(bf16[128,1152]{1,0:T(8,128)(2,1)S(1)} %slice.177), channel_id=1, source_target_pairs={{0,8},{8,0},{16,24},{24,16},{1,9},{9,1},{17,25},{25,17},{2,10},{10... | collective-permute-start | bytes 884744 | tf_op jit(solution)/shard_map/ppermute | solution.py:242
  211.7 10.4 %collective-permute-start.21 = (bf16[128,1152]{1,0:T(8,128)(2,1)S(1)}, bf16[128,1152]{1,0:T(8,128)(2,1)S(1)}, u32[]{:S(2)}, u32[]{:S(2)}) collective-permute-start(bf16[128,1152]{1,0:T(8,128)(2,1)S(1)} %slice.171), channel_id=1, source_target_pairs={{0,16},{8,24},{16,0},{24,8},{1,17},{9,25},{17,1},{25,9},{2,18},{10... | collective-permute-start | bytes 884744 | tf_op jit(solution)/shard_map/ppermute | solution.py:242
  217.2 6.7 %collective-permute-start.23 = (bf16[128,1152]{1,0:T(8,128)(2,1)S(1)}, bf16[128,1152]{1,0:T(8,128)(2,1)S(1)}, u32[]{:S(2)}, u32[]{:S(2)}) collective-permute-start(bf16[128,1152]{1,0:T(8,128)(2,1)S(1)} %slice.173), channel_id=1, source_target_pairs={{0,8},{8,0},{16,24},{24,16},{1,9},{9,1},{17,25},{25,17},{2,10},{10... | collective-permute-start | bytes 884744 | tf_op jit(solution)/shard_map/ppermute | solution.py:242
  224.1 1.2 copy-start.4
  225.7 12.1 %collective-permute-start.9 = (bf16[128,1024]{1,0:T(8,128)(2,1)S(1)}, bf16[128,1024]{1,0:T(8,128)(2,1)S(1)}, u32[]{:S(2)}, u32[]{:S(2)}) collective-permute-start(bf16[128,1024]{1,0:T(8,128)(2,1)S(1)} %get-tuple-element.65), channel_id=1, source_target_pairs={{0,2},{1,3},{2,4},{3,5},{4,6},{5,7},{6,0},{7,1},{8,10},{9,11},{10,... | collective-permute-start | bytes 786440 | tf_op jit(solution)/shard_map/ppermute | solution.py:53
  225.7 17.9 %collective-permute-start.11 = (bf16[128,1024]{1,0:T(8,128)(2,1)S(1)}, bf16[128,1024]{1,0:T(8,128)(2,1)S(1)}, u32[]{:S(2)}, u32[]{:S(2)}) collective-permute-start(bf16[128,1024]{1,0:T(8,128)(2,1)S(1)} %get-tuple-element.66), channel_id=1, source_target_pairs={{0,6},{1,7},{2,0},{3,1},{4,2},{5,3},{6,4},{7,5},{8,14},{9,15},{10,... | collective-permute-start | bytes 786440 | tf_op jit(solution)/shard_map/ppermute | solution.py:53
  229.5 28.7 %collective-permute-start.10 = (bf16[128,1024]{1,0:T(8,128)(2,1)S(1)}, bf16[128,1024]{1,0:T(8,128)(2,1)S(1)}, u32[]{:S(2)}, u32[]{:S(2)}) collective-permute-start(bf16[128,1024]{1,0:T(8,128)(2,1)S(1)} %get-tuple-element.67), channel_id=1, source_target_pairs={{0,4},{1,5},{2,6},{3,7},{4,0},{5,1},{6,2},{7,3},{8,12},{9,13},{10,... | collective-permute-start | bytes 786440 | tf_op jit(solution)/shard_map/ppermute | solution.py:53
  232.1 1.5 copy-start.5
  233.9 25.2 %collective-permute-start.17 = (bf16[128,1024]{1,0:T(8,128)(2,1)S(1)}, bf16[128,1024]{1,0:T(8,128)(2,1)S(1)}, u32[]{:S(2)}, u32[]{:S(2)}) collective-permute-start(bf16[128,1024]{1,0:T(8,128)(2,1)S(1)} %get-tuple-element.62), channel_id=1, source_target_pairs={{0,2},{1,3},{2,4},{3,5},{4,6},{5,7},{6,0},{7,1},{8,10},{9,11},{10,... | collective-permute-start | bytes 786440 | tf_op jit(solution)/shard_map/ppermute | solution.py:53
  234.5 24.6 %collective-permute-start.19 = (bf16[128,1024]{1,0:T(8,128)(2,1)S(1)}, bf16[128,1024]{1,0:T(8,128)(2,1)S(1)}, u32[]{:S(2)}, u32[]{:S(2)}) collective-permute-start(bf16[128,1024]{1,0:T(8,128)(2,1)S(1)} %get-tuple-element.63), channel_id=1, source_target_pairs={{0,6},{1,7},{2,0},{3,1},{4,2},{5,3},{6,4},{7,5},{8,14},{9,15},{10,... | collective-permute-start | bytes 786440 | tf_op jit(solution)/shard_map/ppermute | solution.py:53
  237.8 32.6 %collective-permute-start.18 = (bf16[128,1024]{1,0:T(8,128)(2,1)S(1)}, bf16[128,1024]{1,0:T(8,128)(2,1)S(1)}, u32[]{:S(2)}, u32[]{:S(2)}) collective-permute-start(bf16[128,1024]{1,0:T(8,128)(2,1)S(1)} %get-tuple-element.64), channel_id=1, source_target_pairs={{0,4},{1,5},{2,6},{3,7},{4,0},{5,1},{6,2},{7,3},{8,12},{9,13},{10,... | collective-permute-start | bytes 786440 | tf_op jit(solution)/shard_map/ppermute | solution.py:53
